TPU v7x, 32 devices: a whole 2x2x4 slice. The times are simulated.
32 devices in a mesh: rows: 8 (over z, x), chan: 4 (over y, core).
Axes of the slice: x: 2, y: 2, z: 4, core: 2. Of those that a mesh axis runs over, the one named last changes fastest.
Arguments:
- frames: bfloat16 [9, 32, 480, 256], P(None, 'rows', 'chan'), may hold values from -450 to 450
- spatial_weight: bfloat16 [256, 2304], P('rows'), may hold values from -0.125 to 0.125
- temporal_weight: bfloat16 [256, 768], P('rows'), may hold values from -0.21875 to 0.21875
- down_weight: bfloat16 [256, 2304], P('rows'), may hold values from -0.125 to 0.125
- norm_gain: float32 [256], replicated, may hold values from 0.5 to 1.5
- norm_shift: float32 [256], replicated, may hold values from -3 to 3
- down_bias: float32 [256], replicated, may hold values from -3 to 3
Outputs:
- latent: bfloat16 [9, 16, 240, 256], P(None, 'rows', 'chan')
All inputs are finite; a program needn't handle non-finite values.
Results may differ from a plain program's by a relative error of at most 0.0053.
Values may be sent and summed in bfloat16 or wider, within the bound.
No kernel may reach another device: no remote copies, remote signals or barrier semaphores. Data moves between devices by JAX's collectives and lax.ppermute only.
A program may use at most 128 MiB of HBM per device.

v0:
```python
import jax
import jax.numpy as jnp
from jax import lax
from jax.sharding import PartitionSpec as P

GROUPS = 32
epsilon = 1e-06


def extended_2(cells, sides, width):
    for axis, dim in sides:
        count = lax.axis_size(axis)
        ends = count - 1
        head = lax.slice_in_dim(cells, 0, width, axis=dim)
        tail = lax.slice_in_dim(cells, cells.shape[dim] - width, cells.shape[dim], axis=dim)
        cells = jnp.concatenate(
            [
                lax.ppermute(tail, axis, [(i, (i + 1) % count) for i in range(ends)]),
                cells,
                lax.ppermute(head, axis, [((i + 1) % count, i) for i in range(ends)]),
            ],
            axis=dim,
        )
    return cells


def passed_along(block, axis, distance):
    devices = range(lax.axis_size(axis))
    route = [(i - distance, i) for i in devices if i - distance in devices]
    return lax.ppermute(block, axis, route)


def spatial_taps(padded, weight_rows, width_out):
    rows_out = padded.shape[1] - 2
    cols_out = padded.shape[2] - 2
    summed = None
    for tap_index in range(9):
        row_offset = tap_index // 3
        col_offset = tap_index % 3
        window = padded[
            :, row_offset : row_offset + rows_out, col_offset : col_offset + cols_out, :
        ]
        weight_panel = weight_rows[:, tap_index * width_out : (tap_index + 1) * width_out]
        product = jnp.einsum(
            "fijc,co->fijo", window, weight_panel, preferred_element_type=jnp.float32
        )
        summed = product if summed is None else summed + product
    return summed


def temporal_taps(values, weight_rows, width_out):
    frame_count = values.shape[0]
    summed = None
    for tap_index in range(3):
        lag_frames = 2 - tap_index
        if lag_frames > 0:
            delayed = jnp.concatenate(
                [jnp.repeat(values[:1], lag_frames, axis=0), values[: frame_count - lag_frames]],
                axis=0,
            )
        else:
            delayed = values
        weight_panel = weight_rows[:, tap_index * width_out : (tap_index + 1) * width_out]
        product = jnp.einsum(
            "fijc,co->fijo", delayed, weight_panel, preferred_element_type=jnp.float32
        )
        summed = product if summed is None else summed + product
    return summed


def down_taps(extended, weight_rows, width_out):
    rows_out = (extended.shape[1] - 1) // 2
    cols_out = (extended.shape[2] - 1) // 2
    summed = None
    for tap_index in range(9):
        row_offset = tap_index // 3
        col_offset = tap_index % 3
        window = extended[
            :,
            row_offset : row_offset + 2 * rows_out : 2,
            col_offset : col_offset + 2 * cols_out : 2,
            :,
        ]
        weight_panel = weight_rows[:, tap_index * width_out : (tap_index + 1) * width_out]
        product = jnp.einsum(
            "fijc,co->fijo", window, weight_panel, preferred_element_type=jnp.float32
        )
        summed = product if summed is None else summed + product
    return summed


def group_reduce(partial_sums):
    return lax.psum(partial_sums, ("rows", "chan"))


def place_groups(channel_sums, group_width):
    local_sums = channel_sums.reshape(-1, group_width).sum(axis=1)
    return local_sums


def channel_values(group_vector, group_width):
    return jnp.repeat(group_vector, group_width)


def per_device(
    frames, spatial_weight, temporal_weight, down_weight, norm_gain, norm_shift, down_bias
):
    full_spatial, full_temporal, full_down = (
        lax.all_gather(spatial_weight, "rows", axis=0, tiled=True),
        lax.all_gather(temporal_weight, "rows", axis=0, tiled=True),
        lax.all_gather(down_weight, "rows", axis=0, tiled=True),
    )
    channels = full_spatial.shape[0]
    group_width = channels // GROUPS
    frame_count = frames.shape[0]
    rows_dev = frames.shape[1]
    width_all = frames.shape[2] * lax.axis_size("chan")
    cell_count = float(frame_count * rows_dev * lax.axis_size("rows") * width_all * group_width)
    padded = extended_2(frames, (("rows", 1), ("chan", 2)), 1)
    first = spatial_taps(padded, full_spatial, channels).astype(jnp.bfloat16)
    hidden = temporal_taps(first, full_temporal, channels)
    channel_sums = jnp.sum(hidden, axis=(0, 1, 2))
    totals = group_reduce(place_groups(channel_sums, group_width)[None])
    means = totals[0] / cell_count
    chan_mean = channel_values(means, group_width)
    centered = hidden - chan_mean
    spread = group_reduce(
        place_groups(jnp.sum(centered * centered, axis=(0, 1, 2)), group_width)[None]
    )
    variance = spread[0] / cell_count
    chan_var = channel_values(variance, group_width)
    act = jax.nn.silu(centered * lax.rsqrt(chan_var + epsilon) * norm_gain + norm_shift).astype(
        jnp.bfloat16
    )
    below = passed_along(act[:, :1], "rows", -1)
    extended = jnp.concatenate([act, below], axis=1)
    beside = passed_along(extended[:, :, :1], "chan", -1)
    extended = jnp.concatenate([extended, beside], axis=2)
    latent = down_taps(extended, full_down, channels) + down_bias
    return latent.astype(jnp.bfloat16)


def solution(mesh):
    placed = (
        P(None, "rows", "chan", None),
        P("rows", None),
        P("rows", None),
        P("rows", None),
        P(),
        P(),
        P(),
    )
    return jax.shard_map(
        per_device,
        mesh=mesh,
        in_specs=placed,
        out_specs=P(None, "rows", "chan", None),
        check_vma=False,
    )
```

profile of v0, /device:TPU:3, one launch (start us, length us, event | category | flops | bytes accessed | tf_op | source)
XLA Modules:
  0.0 319.5 jit_solution(4577024968184721207)
XLA Ops:
  7.3 2.1 fusion.64
  9.4 3.2 collective-permute-start
  12.6 2.9 collective-permute-start.1
  15.5 22.7 %collective-permute-done = bf16[9,1,120,256]{3,2,1,0:T(8,128)(2,1)} collective-permute-done((bf16[9,1,120,256]{3,2,1,0:T(8,128)(2,1)S(1)}, bf16[9,1,120,256]{3,2,1,0:T(8,128)(2,1)}, u32[]{:S(2)}, u32[]{:S(2)}) %collective-permute-start) | collective-permute-done | bytes 552992 | tf_op jit(solution)/shard_map/ppermute | solution.py:18
  42.3 4.6 %collective-permute-start.2 = (bf16[9,6,1,256]{3,2,1,0:T(2,128)(2,1)S(1)}, bf16[9,6,1,256]{3,2,1,0:T(2,128)(2,1)S(1)}, u32[]{:S(2)}, u32[]{:S(2)}) collective-permute-start(bf16[9,6,1,256]{3,2,1,0:T(2,128)(2,1)S(1)} %get-tuple-element.6), channel_id=1, source_target_pairs={{0,1},{1,2},{2,3},{4,5},{5,6},{6,7},{8,9},{9,10},{10,11},{12,13},{... | collective-permute-start | bytes 82952 | tf_op jit(solution)/shard_map/ppermute | solution.py:18
  46.9 25.9 %all_gather.10 = bf16[256,768]{1,0:T(8,128)(2,1)} all-gather(bf16[32,768]{1,0:T(8,128)(2,1)S(1)} %copy-done.12), channel_id=1, replica_groups=mesh['rows'=8,'chan'=4] {'rows'}, dimensions={0}, use_global_device_ids=true | all-gather | bytes 442368 | tf_op jit(solution)/shard_map/all_gather | solution.py:110
  72.8 5.5 %collective-permute-start.3 = (bf16[9,6,1,256]{3,2,1,0:T(2,128)(2,1)S(1)}, bf16[9,6,1,256]{3,2,1,0:T(2,128)(2,1)S(1)}, u32[]{:S(2)}, u32[]{:S(2)}) collective-permute-start(bf16[9,6,1,256]{3,2,1,0:T(2,128)(2,1)S(1)} %get-tuple-element.5), channel_id=1, source_target_pairs={{1,0},{2,1},{3,2},{5,4},{6,5},{7,6},{9,8},{10,9},{11,10},{13,12},{... | collective-permute-start | bytes 82952 | tf_op jit(solution)/shard_map/ppermute | solution.py:20
  78.4 3.8 %fusion.15 = f32[9,4,120,256]{3,2,1,0:T(8,128)} fusion(bf16[9,6,120,256]{3,2,1,0:T(8,128)(2,1)S(1)} %constant_dynamic-update-slice_fusion, bf16[9,6,1,256]{3,2,1,0:T(2,128)(2,1)S(1)} %collective-permute-done.2, bf16[256,2304]{1,0:T(8,128)(2,1)} %all-gather.3.cloned.1.call-done), kind=kOutput, calls=%fused_computation.29 | convolution fusion | flops 570654720 | bytes 7900160 | tf_op jit(solution)/shard_map/fijc,co->fijo/dot_general | solution.py:44
  82.2 2.9 fusion.18
  85.1 2.8 fusion.12
  87.8 2.9 fusion.9
  90.8 2.9 fusion.22
  93.6 3.9 %fusion = f32[9,4,120,256]{3,2,1,0:T(8,128)} fusion(bf16[9,4,120,256]{3,2,1,0:T(8,128)(2,1)S(1)} %copy-done, bf16[9,1,120,256]{3,2,1,0:T(8,128)(2,1)} %collective-permute-done, bf16[256,2304]{1,0:T(8,128)(2,1)S(1)} %copy-done.11), kind=kOutput, calls=%fused_computation.15 | convolution fusion | flops 571760640 | bytes 7319552 | tf_op jit(solution)/shard_map/fijc,co->fijo/dot_general | solution.py:44
  99.3 2.9 fusion.50
  102.2 12.6 %add_convert_fusion = bf16[9,4,120,256]{3,2,1,0:T(8,128)(2,1)} fusion(f32[9,4,120,256]{3,2,1,0:T(8,128)S(1)} %fusion.4, f32[9,4,120,256]{3,2,1,0:T(8,128)} %fusion.22, f32[9,4,120,256]{3,2,1,0:T(8,128)} %fusion.9, f32[9,4,120,256]{3,2,1,0:T(8,128)} %fusion.50, f32[9,4,120,256]{3,2,1,0:T(8,128)} %fusion.15, f32[9,4,120,256]{3,2,1,0:T(8,128)} %fusion.12, ...), kind=kOutput, calls=%fused_computation.7 | convolution fusion | flops 580608000 | bytes 41105408 | tf_op jit(solution)/shard_map/fijc,co->fijo/dot_general | solution.py:44
  120.4 3.0 fusion.65
  123.7 38.6 %psum.14 = f32[1,32]{1,0:T(1,128)S(1)} all-reduce(f32[1,32]{1,0:T(1,128)S(1)} %bitcast.127), channel_id=1, replica_groups=mesh['rows'=8,'chan'=4] {'rows','chan'}, use_global_device_ids=true, to_apply=%region_2.0 | all-reduce | flops 32 | bytes 256 | tf_op jit(solution)/shard_map/psum | solution.py:93
  162.5 2.9 multiply_reduce_fusion
  165.5 41.8 %psum.15 = f32[1,32]{1,0:T(1,128)S(1)} all-reduce(f32[1,32]{1,0:T(1,128)S(1)} %bitcast.126), channel_id=1, replica_groups=mesh['rows'=8,'chan'=4] {'rows','chan'}, use_global_device_ids=true, to_apply=%region_5.0 | all-reduce | flops 32 | bytes 256 | tf_op jit(solution)/shard_map/psum | solution.py:93
  207.5 3.6 %multiply_convert_fusion = bf16[9,4,120,256]{3,2,1,0:T(8,128)(2,1)S(1)} fusion(f32[9,4,120,256]{3,2,1,0:T(8,128)} %get-tuple-element.12, f32[256]{0:T(256)S(1)} %copy-done.13, f32[256]{0:T(256)S(1)} %copy-done.14, f32[256]{0:T(256)S(1)} %rsqrt.16, f32[256]{0:T(256)S(1)} %sub.10), kind=kLoop, calls=%fused_computation.4 | loop fusion | flops 9953280 | bytes 6639616 | tf_op jit(solution)/shard_map/convert_element_type | solution.py:132
  214.8 2.2 fusion.48
  217.1 10.4 %collective-permute-done.4 = bf16[9,1,120,256]{3,2,1,0:T(8,128)(2,1)S(1)} collective-permute-done((bf16[9,1,120,256]{3,2,1,0:T(8,128)(2,1)}, bf16[9,1,120,256]{3,2,1,0:T(8,128)(2,1)S(1)}, u32[]{:S(2)}, u32[]{:S(2)}) %collective-permute-start.4) | collective-permute-done | bytes 552992 | tf_op jit(solution)/shard_map/ppermute | solution.py:30
  229.3 10.3 %slice.188 = bf16[9,2,60,256]{3,2,1,0:T(8,128)(2,1)} slice(bf16[9,5,120,256]{3,2,1,0:T(8,128)(2,1)} %pad_maximum_fusion), slice={[0:9:1], [1:5:2], [0:120:2], [0:256:1]} | slice | bytes 1105920 | tf_op jit(solution)/shard_map/slice | solution.py:78
  239.6 8.5 %slice.194 = bf16[9,2,60,256]{3,2,1,0:T(8,128)(2,1)S(1)} slice(bf16[9,5,120,256]{3,2,1,0:T(8,128)(2,1)} %pad_maximum_fusion), slice={[0:9:1], [2:5:2], [0:120:2], [0:256:1]} | slice | bytes 1105920 | tf_op jit(solution)/shard_map/slice | solution.py:78
  248.2 4.5 %collective-permute-start.5 = (bf16[9,5,1,256]{3,2,1,0:T(2,128)(2,1)S(1)}, bf16[9,5,1,256]{3,2,1,0:T(2,128)(2,1)S(1)}, u32[]{:S(2)}, u32[]{:S(2)}) collective-permute-start(bf16[9,5,1,256]{3,2,1,0:T(2,128)(2,1)S(1)} %fusion.51), channel_id=1, source_target_pairs={{1,0},{2,1},{3,2},{5,4},{6,5},{7,6},{9,8},{10,9},{11,10},{13,12},{... | collective-permute-start | bytes 69128 | tf_op jit(solution)/shard_map/ppermute | solution.py:30
  252.7 2.3 fusion.47
  254.9 2.2 fusion.44
  259.2 10.5 %slice.184 = bf16[9,2,60,256]{3,2,1,0:T(8,128)(2,1)} slice(bf16[9,5,121,256]{3,2,1,0:T(8,128)(2,1)} %pad_maximum_fusion.1), slice={[0:9:1], [0:4:2], [1:121:2], [0:256:1]} | slice | bytes 1105920 | tf_op jit(solution)/shard_map/slice | solution.py:78
  269.6 10.2 %slice.198 = bf16[9,2,60,256]{3,2,1,0:T(8,128)(2,1)} slice(bf16[9,5,121,256]{3,2,1,0:T(8,128)(2,1)} %pad_maximum_fusion.1), slice={[0:9:1], [2:5:2], [2:121:2], [0:256:1]} | slice | bytes 1105920 | tf_op jit(solution)/shard_map/slice | solution.py:78
  279.8 10.1 %slice.196 = bf16[9,2,60,256]{3,2,1,0:T(8,128)(2,1)} slice(bf16[9,5,121,256]{3,2,1,0:T(8,128)(2,1)} %pad_maximum_fusion.1), slice={[0:9:1], [2:5:2], [1:121:2], [0:256:1]} | slice | bytes 1105920 | tf_op jit(solution)/shard_map/slice | solution.py:78
  289.9 6.0 %slice.192 = bf16[9,2,60,256]{3,2,1,0:T(8,128)(2,1)} slice(bf16[9,5,121,256]{3,2,1,0:T(8,128)(2,1)S(1)} %copy-done.2), slice={[0:9:1], [1:5:2], [2:121:2], [0:256:1]} | slice | bytes 1105920 | tf_op jit(solution)/shard_map/slice | solution.py:78
  295.9 5.9 %slice.190 = bf16[9,2,60,256]{3,2,1,0:T(8,128)(2,1)} slice(bf16[9,5,121,256]{3,2,1,0:T(8,128)(2,1)S(1)} %copy-done.2), slice={[0:9:1], [1:5:2], [1:121:2], [0:256:1]} | slice | bytes 1105920 | tf_op jit(solution)/shard_map/slice | solution.py:78
  (79 shorter events, 31.2 us)
Async XLA Ops:
  6.5 71.8 %all-gather.3.cloned.1.call-start = ((), (), s32[]{:S(2)}) async-start(), calls=%async_computation | async-start | bytes 1327104 | tf_op jit(solution)/shard_map/all_gather | solution.py:109
  7.3 207.6 %all-gather.5.cloned.1.call-start = ((), (), s32[]{:S(2)}) async-start(), calls=%async_computation.1 | async-start | bytes 1327104 | tf_op jit(solution)/shard_map/all_gather | solution.py:111
  9.4 28.8 %collective-permute-start = (bf16[9,1,120,256]{3,2,1,0:T(8,128)(2,1)S(1)}, bf16[9,1,120,256]{3,2,1,0:T(8,128)(2,1)}, u32[]{:S(2)}, u32[]{:S(2)}) collective-permute-start(bf16[9,1,120,256]{3,2,1,0:T(8,128)(2,1)S(1)} %get-tuple-element.9), channel_id=1, source_target_pairs={{0,4},{4,8},{8,12},{12,16},{16,20},{20,24},{24,28},{1,5},{5,9},{9,... | collective-permute-start | bytes 1658888 | tf_op jit(solution)/shard_map/ppermute | solution.py:18
  12.6 28.5 %collective-permute-start.1 = (bf16[9,1,120,256]{3,2,1,0:T(8,128)(2,1)}, bf16[9,1,120,256]{3,2,1,0:T(8,128)(2,1)}, u32[]{:S(2)}, u32[]{:S(2)}) collective-permute-start(bf16[9,1,120,256]{3,2,1,0:T(8,128)(2,1)} %get-tuple-element.10), channel_id=1, source_target_pairs={{4,0},{8,4},{12,8},{16,12},{20,16},{24,20},{28,24},{5,1},{9,5},{13... | collective-permute-start | bytes 1658888 | tf_op jit(solution)/shard_map/ppermute | solution.py:20
  39.3 7.6 %copy-start.12 = (bf16[32,768]{1,0:T(8,128)(2,1)S(1)}, bf16[32,768]{1,0:T(8,128)(2,1)}, u32[]{:S(2)}) copy-start(bf16[32,768]{1,0:T(8,128)(2,1)} %param.9) | copy-start | bytes 147460
  42.3 36.0 %collective-permute-start.2 = (bf16[9,6,1,256]{3,2,1,0:T(2,128)(2,1)S(1)}, bf16[9,6,1,256]{3,2,1,0:T(2,128)(2,1)S(1)}, u32[]{:S(2)}, u32[]{:S(2)}) collective-permute-start(bf16[9,6,1,256]{3,2,1,0:T(2,128)(2,1)S(1)} %get-tuple-element.6), channel_id=1, source_target_pairs={{0,1},{1,2},{2,3},{4,5},{5,6},{6,7},{8,9},{9,10},{10,11},{12,13},{... | collective-permute-start | bytes 82952 | tf_op jit(solution)/shard_map/ppermute | solution.py:18
  72.8 12.3 %collective-permute-start.3 = (bf16[9,6,1,256]{3,2,1,0:T(2,128)(2,1)S(1)}, bf16[9,6,1,256]{3,2,1,0:T(2,128)(2,1)S(1)}, u32[]{:S(2)}, u32[]{:S(2)}) collective-permute-start(bf16[9,6,1,256]{3,2,1,0:T(2,128)(2,1)S(1)} %get-tuple-element.5), channel_id=1, source_target_pairs={{1,0},{2,1},{3,2},{5,4},{6,5},{7,6},{9,8},{10,9},{11,10},{13,12},{... | collective-permute-start | bytes 82952 | tf_op jit(solution)/shard_map/ppermute | solution.py:20
  78.4 3.8 %copy-start.11 = (bf16[256,2304]{1,0:T(8,128)(2,1)S(1)}, bf16[256,2304]{1,0:T(8,128)(2,1)}, u32[]{:S(2)}) copy-start(bf16[256,2304]{1,0:T(8,128)(2,1)} %all-gather.3.cloned.1.call-done) | copy-start | bytes 3538948
  90.8 2.9 copy-start
  114.8 1.6 copy-start.1
  116.4 1.0 copy-start.10
  117.4 1.5 slice-start
  118.9 1.5 slice-start.1
  123.5 84.1 %copy-start.13 = (f32[256]{0:T(256)S(1)}, f32[256]{0:T(256)}, u32[]{:S(2)}) copy-start(f32[256]{0:T(256)} %param.12) | copy-start | bytes 3076
  123.5 84.1 %copy-start.14 = (f32[256]{0:T(256)S(1)}, f32[256]{0:T(256)}, u32[]{:S(2)}) copy-start(f32[256]{0:T(256)} %param.11) | copy-start | bytes 3076
  212.0 15.5 %collective-permute-start.4 = (bf16[9,1,120,256]{3,2,1,0:T(8,128)(2,1)}, bf16[9,1,120,256]{3,2,1,0:T(8,128)(2,1)S(1)}, u32[]{:S(2)}, u32[]{:S(2)}) collective-permute-start(bf16[9,1,120,256]{3,2,1,0:T(8,128)(2,1)} %slice.226), channel_id=1, source_target_pairs={{4,0},{8,4},{12,8},{16,12},{20,16},{24,20},{28,24},{5,1},{9,5},{13... | collective-permute-start | bytes 1658888 | tf_op jit(solution)/shard_map/ppermute | solution.py:30
  248.1 4.6 %copy-start.8 = (bf16[9,2,60,256]{3,2,1,0:T(8,128)(2,1)S(1)}, bf16[9,2,60,256]{3,2,1,0:T(8,128)(2,1)}, u32[]{:S(2)}) copy-start(bf16[9,2,60,256]{3,2,1,0:T(8,128)(2,1)} %slice.188) | copy-start | bytes 1658884
  248.2 9.0 %collective-permute-start.5 = (bf16[9,5,1,256]{3,2,1,0:T(2,128)(2,1)S(1)}, bf16[9,5,1,256]{3,2,1,0:T(2,128)(2,1)S(1)}, u32[]{:S(2)}, u32[]{:S(2)}) collective-permute-start(bf16[9,5,1,256]{3,2,1,0:T(2,128)(2,1)S(1)} %fusion.51), channel_id=1, source_target_pairs={{1,0},{2,1},{3,2},{5,4},{6,5},{7,6},{9,8},{10,9},{11,10},{13,12},{... | collective-permute-start | bytes 69128 | tf_op jit(solution)/shard_map/ppermute | solution.py:30
  259.2 30.7 %copy-start.2 = (bf16[9,5,121,256]{3,2,1,0:T(8,128)(2,1)S(1)}, bf16[9,5,121,256]{3,2,1,0:T(8,128)(2,1)}, u32[]{:S(2)}) copy-start(bf16[9,5,121,256]{3,2,1,0:T(8,128)(2,1)} %pad_maximum_fusion.1) | copy-start | bytes 8363524
  302.8 3.1 copy-start.9
  302.8 4.3 %copy-start.7 = (bf16[9,2,60,256]{3,2,1,0:T(8,128)(2,1)S(1)}, bf16[9,2,60,256]{3,2,1,0:T(8,128)(2,1)}, u32[]{:S(2)}) copy-start(bf16[9,2,60,256]{3,2,1,0:T(8,128)(2,1)} %slice.190) | copy-start | bytes 1658884
  304.3 4.2 %copy-start.5 = (f32[9,2,60,256]{3,2,1,0:T(8,128)S(1)}, f32[9,2,60,256]{3,2,1,0:T(8,128)}, u32[]{:S(2)}) copy-start(f32[9,2,60,256]{3,2,1,0:T(8,128)} %fusion.48) | copy-start | bytes 3317764
  304.3 4.2 %copy-start.6 = (bf16[9,2,60,256]{3,2,1,0:T(8,128)(2,1)S(1)}, bf16[9,2,60,256]{3,2,1,0:T(8,128)(2,1)}, u32[]{:S(2)}) copy-start(bf16[9,2,60,256]{3,2,1,0:T(8,128)(2,1)} %slice.184) | copy-start | bytes 1658884
  307.1 2.6 copy-start.3
  307.1 2.6 copy-start.4
  307.1 2.6 copy-start.15
Sparse Core Ops, SparseCore 0:
  9.5 52.3 all-gather.2
  64.2 39.7 all-gather.4
where the time goes:
time: 322 us; the launch traced here: 320 us
  blocking collectives  106 us (33%)
  local copies, waits for them, and re-layouts  76.4 us (24%)
  matrix products  56 us (17%)
  waiting for transfers between devices  33.9 us (11%)
  starting transfers between devices  22.6 us (7%)
  between operations  13.8 us (4%)
  other arithmetic  10.5 us (3%)
    psum x2, blocking collectives, group_reduce(): return lax.psum(partial_sums, ('rows', 'chan'))  80.4 us
    slice x9, local copies, waits for them, and re-layouts, down_taps(): extended[:, row_offset:row_offset + 2 * rows_out:2, col_offset:col_offset...  63.3 us
    dot_general x9, matrix products, spatial_taps(): jnp.einsum('fijc,co->fijo', window, weight_panel, preferred_element_type=...  36.4 us
    all_gather x1, blocking collectives, per_device(): lax.all_gather(temporal_weight, 'rows', axis=0, tiled=True)  25.9 us
    ppermute x2, waiting for transfers between devices, extended_2(): lax.ppermute(tail, axis, [(i, (i + 1) % count) for i in range(ends)])  22.7 us
    dot_general x9, matrix products, down_taps(): jnp.einsum('fijc,co->fijo', window, weight_panel, preferred_element_type=...  15.1 us
    ppermute x2, waiting for transfers between devices, passed_along(): return lax.ppermute(block, axis, route)  10.4 us
    ppermute x2, starting transfers between devices, extended_2(): lax.ppermute(head, axis, [((i + 1) % count, i) for i in range(ends)])  8.43 us
  transfers between devices with their start and end apart: 8, of which 2 were waited for; matrix products, arithmetic and copies ran while one was open for 20% of the time, Pallas kernels for 0%

commit v1 on v0

--- a/solution.py
+++ b/solution.py
@@ -90,7 +90,7 @@
 
 
 def group_reduce(partial_sums):
-    return lax.psum(partial_sums, ("rows", "chan"))
+    return jnp.sum(lax.all_gather(partial_sums, ("rows", "chan")), axis=0)
 
 
 def place_groups(channel_sums, group_width):

time: 322 us -> 322 us (level)
    psum x2 -> x0, blocking collectives: 80.4 us -> none  [group_reduce(): return lax.psum(partial_sums, ('rows', 'chan'))]
    unnamed x0 -> x2, blocking collectives: none -> 80.4 us
where the time goes in v1:
time: 322 us; the launch traced here: 320 us
  blocking collectives  106 us (33%)
  local copies, waits for them, and re-layouts  77 us (24%)
  matrix products  55.8 us (17%)
  waiting for transfers between devices  33.9 us (11%)
  starting transfers between devices  22.6 us (7%)
  between operations  13.8 us (4%)
  other arithmetic  10.6 us (3%)
    unnamed x2, blocking collectives  80.4 us
    slice x9, local copies, waits for them, and re-layouts, down_taps(): extended[:, row_offset:row_offset + 2 * rows_out:2, col_offset:col_offset...  63.3 us
    dot_general x9, matrix products, spatial_taps(): jnp.einsum('fijc,co->fijo', window, weight_panel, preferred_element_type=...  36.3 us
    all_gather x1, blocking collectives, per_device(): lax.all_gather(temporal_weight, 'rows', axis=0, tiled=True)  25.9 us
    ppermute x2, waiting for transfers between devices, extended_2(): lax.ppermute(tail, axis, [(i, (i + 1) % count) for i in range(ends)])  22.7 us
    dot_general x9, matrix products, down_taps(): jnp.einsum('fijc,co->fijo', window, weight_panel, preferred_element_type=...  15 us
    ppermute x2, waiting for transfers between devices, passed_along(): return lax.ppermute(block, axis, route)  10.4 us
    ppermute x2, starting transfers between devices, extended_2(): lax.ppermute(head, axis, [((i + 1) % count, i) for i in range(ends)])  8.43 us
  transfers between devices with their start and end apart: 8, of which 2 were waited for; matrix products, arithmetic and copies ran while one was open for 20% of the time, Pallas kernels for 0%

profile of v1, /device:TPU:3, one launch (start us, length us, event | category | flops | bytes accessed | tf_op | source)
XLA Modules:
  0.0 320.0 jit_solution(2556117927788334304)
XLA Ops:
  7.3 2.1 fusion.64
  9.4 3.2 collective-permute-start
  12.6 2.9 collective-permute-start.1
  15.5 22.7 %collective-permute-done = bf16[9,1,120,256]{3,2,1,0:T(8,128)(2,1)} collective-permute-done((bf16[9,1,120,256]{3,2,1,0:T(8,128)(2,1)S(1)}, bf16[9,1,120,256]{3,2,1,0:T(8,128)(2,1)}, u32[]{:S(2)}, u32[]{:S(2)}) %collective-permute-start) | collective-permute-done | bytes 552992 | tf_op jit(solution)/shard_map/ppermute | solution.py:18
  42.3 4.6 %collective-permute-start.2 = (bf16[9,6,1,256]{3,2,1,0:T(2,128)(2,1)S(1)}, bf16[9,6,1,256]{3,2,1,0:T(2,128)(2,1)S(1)}, u32[]{:S(2)}, u32[]{:S(2)}) collective-permute-start(bf16[9,6,1,256]{3,2,1,0:T(2,128)(2,1)S(1)} %get-tuple-element.6), channel_id=1, source_target_pairs={{0,1},{1,2},{2,3},{4,5},{5,6},{6,7},{8,9},{9,10},{10,11},{12,13},{... | collective-permute-start | bytes 82952 | tf_op jit(solution)/shard_map/ppermute | solution.py:18
  46.9 25.9 %all_gather.16 = bf16[256,768]{1,0:T(8,128)(2,1)} all-gather(bf16[32,768]{1,0:T(8,128)(2,1)S(1)} %copy-done.12), channel_id=1, replica_groups=mesh['rows'=8,'chan'=4] {'rows'}, dimensions={0}, use_global_device_ids=true | all-gather | bytes 442368 | tf_op jit(solution)/shard_map/all_gather | solution.py:110
  72.8 5.5 %collective-permute-start.3 = (bf16[9,6,1,256]{3,2,1,0:T(2,128)(2,1)S(1)}, bf16[9,6,1,256]{3,2,1,0:T(2,128)(2,1)S(1)}, u32[]{:S(2)}, u32[]{:S(2)}) collective-permute-start(bf16[9,6,1,256]{3,2,1,0:T(2,128)(2,1)S(1)} %get-tuple-element.5), channel_id=1, source_target_pairs={{1,0},{2,1},{3,2},{5,4},{6,5},{7,6},{9,8},{10,9},{11,10},{13,12},{... | collective-permute-start | bytes 82952 | tf_op jit(solution)/shard_map/ppermute | solution.py:20
  78.4 3.8 %fusion.15 = f32[9,4,120,256]{3,2,1,0:T(8,128)} fusion(bf16[9,6,120,256]{3,2,1,0:T(8,128)(2,1)S(1)} %constant_dynamic-update-slice_fusion, bf16[9,6,1,256]{3,2,1,0:T(2,128)(2,1)S(1)} %collective-permute-done.2, bf16[256,2304]{1,0:T(8,128)(2,1)} %all-gather.5.cloned.1.call-done), kind=kOutput, calls=%fused_computation.29 | convolution fusion | flops 570654720 | bytes 7900160 | tf_op jit(solution)/shard_map/fijc,co->fijo/dot_general | solution.py:44
  82.2 2.8 fusion.18
  85.0 2.8 fusion.12
  87.8 2.9 fusion.9
  90.7 2.9 fusion.22
  93.6 3.9 %fusion = f32[9,4,120,256]{3,2,1,0:T(8,128)} fusion(bf16[9,4,120,256]{3,2,1,0:T(8,128)(2,1)S(1)} %copy-done, bf16[9,1,120,256]{3,2,1,0:T(8,128)(2,1)} %collective-permute-done, bf16[256,2304]{1,0:T(8,128)(2,1)S(1)} %copy-done.11), kind=kOutput, calls=%fused_computation.15 | convolution fusion | flops 571760640 | bytes 7319552 | tf_op jit(solution)/shard_map/fijc,co->fijo/dot_general | solution.py:44
  99.2 2.9 fusion.50
  102.1 12.6 %add_convert_fusion = bf16[9,4,120,256]{3,2,1,0:T(8,128)(2,1)} fusion(f32[9,4,120,256]{3,2,1,0:T(8,128)S(1)} %fusion.4, f32[9,4,120,256]{3,2,1,0:T(8,128)} %fusion.22, f32[9,4,120,256]{3,2,1,0:T(8,128)} %fusion.9, f32[9,4,120,256]{3,2,1,0:T(8,128)} %fusion.50, f32[9,4,120,256]{3,2,1,0:T(8,128)} %fusion.15, f32[9,4,120,256]{3,2,1,0:T(8,128)} %fusion.12, ...), kind=kOutput, calls=%fused_computation.7 | convolution fusion | flops 580608000 | bytes 41105408 | tf_op jit(solution)/shard_map/fijc,co->fijo/dot_general | solution.py:44
  120.3 3.0 fusion.65
  123.8 38.8 %all-reduce = f32[1024]{0:T(1024)S(1)} all-reduce(f32[1024]{0:T(1024)S(1)} %dynamic-update-slice), channel_id=2, replica_groups=mesh['rows'=8,'chan'=4] {'rows','chan'}, use_global_device_ids=true, to_apply=%add | all-reduce | flops 1024 | bytes 8192
  162.8 2.9 multiply_reduce_fusion
  166.1 41.6 %all-reduce.1 = f32[1024]{0:T(1024)S(1)} all-reduce(f32[1024]{0:T(1024)S(1)} %dynamic-update-slice.1), channel_id=3, replica_groups=mesh['rows'=8,'chan'=4] {'rows','chan'}, use_global_device_ids=true, to_apply=%add.1 | all-reduce | flops 1024 | bytes 8192
  208.1 3.6 %multiply_convert_fusion = bf16[9,4,120,256]{3,2,1,0:T(8,128)(2,1)S(1)} fusion(f32[9,4,120,256]{3,2,1,0:T(8,128)} %get-tuple-element.12, f32[256]{0:T(256)S(1)} %copy-done.13, f32[256]{0:T(256)S(1)} %copy-done.14, f32[256]{0:T(256)S(1)} %rsqrt.12, f32[256]{0:T(256)S(1)} %sub.10), kind=kLoop, calls=%fused_computation.4 | loop fusion | flops 9953280 | bytes 6639616 | tf_op jit(solution)/shard_map/convert_element_type | solution.py:132
  215.4 2.2 fusion.48
  217.6 10.4 %collective-permute-done.4 = bf16[9,1,120,256]{3,2,1,0:T(8,128)(2,1)S(1)} collective-permute-done((bf16[9,1,120,256]{3,2,1,0:T(8,128)(2,1)}, bf16[9,1,120,256]{3,2,1,0:T(8,128)(2,1)S(1)}, u32[]{:S(2)}, u32[]{:S(2)}) %collective-permute-start.4) | collective-permute-done | bytes 552992 | tf_op jit(solution)/shard_map/ppermute | solution.py:30
  229.8 10.3 %slice.188 = bf16[9,2,60,256]{3,2,1,0:T(8,128)(2,1)} slice(bf16[9,5,120,256]{3,2,1,0:T(8,128)(2,1)} %pad_maximum_fusion), slice={[0:9:1], [1:5:2], [0:120:2], [0:256:1]} | slice | bytes 1105920 | tf_op jit(solution)/shard_map/slice | solution.py:78
  240.1 8.5 %slice.194 = bf16[9,2,60,256]{3,2,1,0:T(8,128)(2,1)S(1)} slice(bf16[9,5,120,256]{3,2,1,0:T(8,128)(2,1)} %pad_maximum_fusion), slice={[0:9:1], [2:5:2], [0:120:2], [0:256:1]} | slice | bytes 1105920 | tf_op jit(solution)/shard_map/slice | solution.py:78
  248.7 4.5 %collective-permute-start.5 = (bf16[9,5,1,256]{3,2,1,0:T(2,128)(2,1)S(1)}, bf16[9,5,1,256]{3,2,1,0:T(2,128)(2,1)S(1)}, u32[]{:S(2)}, u32[]{:S(2)}) collective-permute-start(bf16[9,5,1,256]{3,2,1,0:T(2,128)(2,1)S(1)} %fusion.51), channel_id=1, source_target_pairs={{1,0},{2,1},{3,2},{5,4},{6,5},{7,6},{9,8},{10,9},{11,10},{13,12},{... | collective-permute-start | bytes 69128 | tf_op jit(solution)/shard_map/ppermute | solution.py:30
  253.2 2.3 fusion.47
  255.5 2.2 fusion.44
  259.7 10.5 %slice.184 = bf16[9,2,60,256]{3,2,1,0:T(8,128)(2,1)} slice(bf16[9,5,121,256]{3,2,1,0:T(8,128)(2,1)} %pad_maximum_fusion.1), slice={[0:9:1], [0:4:2], [1:121:2], [0:256:1]} | slice | bytes 1105920 | tf_op jit(solution)/shard_map/slice | solution.py:78
  270.2 10.1 %slice.198 = bf16[9,2,60,256]{3,2,1,0:T(8,128)(2,1)} slice(bf16[9,5,121,256]{3,2,1,0:T(8,128)(2,1)} %pad_maximum_fusion.1), slice={[0:9:1], [2:5:2], [2:121:2], [0:256:1]} | slice | bytes 1105920 | tf_op jit(solution)/shard_map/slice | solution.py:78
  280.3 10.1 %slice.196 = bf16[9,2,60,256]{3,2,1,0:T(8,128)(2,1)} slice(bf16[9,5,121,256]{3,2,1,0:T(8,128)(2,1)} %pad_maximum_fusion.1), slice={[0:9:1], [2:5:2], [1:121:2], [0:256:1]} | slice | bytes 1105920 | tf_op jit(solution)/shard_map/slice | solution.py:78
  290.4 6.0 %slice.192 = bf16[9,2,60,256]{3,2,1,0:T(8,128)(2,1)} slice(bf16[9,5,121,256]{3,2,1,0:T(8,128)(2,1)S(1)} %copy-done.2), slice={[0:9:1], [1:5:2], [2:121:2], [0:256:1]} | slice | bytes 1105920 | tf_op jit(solution)/shard_map/slice | solution.py:78
  296.4 5.9 %slice.190 = bf16[9,2,60,256]{3,2,1,0:T(8,128)(2,1)} slice(bf16[9,5,121,256]{3,2,1,0:T(8,128)(2,1)S(1)} %copy-done.2), slice={[0:9:1], [1:5:2], [1:121:2], [0:256:1]} | slice | bytes 1105920 | tf_op jit(solution)/shard_map/slice | solution.py:78
  (87 shorter events, 31.9 us)
Async XLA Ops:
  6.5 71.8 %all-gather.5.cloned.1.call-start = ((), (), s32[]{:S(2)}) async-start(), calls=%async_computation | async-start | bytes 1327104 | tf_op jit(solution)/shard_map/all_gather | solution.py:109
  7.3 208.1 %all-gather.7.cloned.1.call-start = ((), (), s32[]{:S(2)}) async-start(), calls=%async_computation.1 | async-start | bytes 1327104 | tf_op jit(solution)/shard_map/all_gather | solution.py:111
  9.4 28.8 %collective-permute-start = (bf16[9,1,120,256]{3,2,1,0:T(8,128)(2,1)S(1)}, bf16[9,1,120,256]{3,2,1,0:T(8,128)(2,1)}, u32[]{:S(2)}, u32[]{:S(2)}) collective-permute-start(bf16[9,1,120,256]{3,2,1,0:T(8,128)(2,1)S(1)} %get-tuple-element.9), channel_id=1, source_target_pairs={{0,4},{4,8},{8,12},{12,16},{16,20},{20,24},{24,28},{1,5},{5,9},{9,... | collective-permute-start | bytes 1658888 | tf_op jit(solution)/shard_map/ppermute | solution.py:18
  12.6 28.5 %collective-permute-start.1 = (bf16[9,1,120,256]{3,2,1,0:T(8,128)(2,1)}, bf16[9,1,120,256]{3,2,1,0:T(8,128)(2,1)}, u32[]{:S(2)}, u32[]{:S(2)}) collective-permute-start(bf16[9,1,120,256]{3,2,1,0:T(8,128)(2,1)} %get-tuple-element.10), channel_id=1, source_target_pairs={{4,0},{8,4},{12,8},{16,12},{20,16},{24,20},{28,24},{5,1},{9,5},{13... | collective-permute-start | bytes 1658888 | tf_op jit(solution)/shard_map/ppermute | solution.py:20
  39.3 7.6 %copy-start.12 = (bf16[32,768]{1,0:T(8,128)(2,1)S(1)}, bf16[32,768]{1,0:T(8,128)(2,1)}, u32[]{:S(2)}) copy-start(bf16[32,768]{1,0:T(8,128)(2,1)} %param.9) | copy-start | bytes 147460
  42.3 36.0 %collective-permute-start.2 = (bf16[9,6,1,256]{3,2,1,0:T(2,128)(2,1)S(1)}, bf16[9,6,1,256]{3,2,1,0:T(2,128)(2,1)S(1)}, u32[]{:S(2)}, u32[]{:S(2)}) collective-permute-start(bf16[9,6,1,256]{3,2,1,0:T(2,128)(2,1)S(1)} %get-tuple-element.6), channel_id=1, source_target_pairs={{0,1},{1,2},{2,3},{4,5},{5,6},{6,7},{8,9},{9,10},{10,11},{12,13},{... | collective-permute-start | bytes 82952 | tf_op jit(solution)/shard_map/ppermute | solution.py:18
  72.8 12.2 %collective-permute-start.3 = (bf16[9,6,1,256]{3,2,1,0:T(2,128)(2,1)S(1)}, bf16[9,6,1,256]{3,2,1,0:T(2,128)(2,1)S(1)}, u32[]{:S(2)}, u32[]{:S(2)}) collective-permute-start(bf16[9,6,1,256]{3,2,1,0:T(2,128)(2,1)S(1)} %get-tuple-element.5), channel_id=1, source_target_pairs={{1,0},{2,1},{3,2},{5,4},{6,5},{7,6},{9,8},{10,9},{11,10},{13,12},{... | collective-permute-start | bytes 82952 | tf_op jit(solution)/shard_map/ppermute | solution.py:20
  78.4 3.8 %copy-start.11 = (bf16[256,2304]{1,0:T(8,128)(2,1)S(1)}, bf16[256,2304]{1,0:T(8,128)(2,1)}, u32[]{:S(2)}) copy-start(bf16[256,2304]{1,0:T(8,128)(2,1)} %all-gather.5.cloned.1.call-done) | copy-start | bytes 3538948
  90.7 2.9 copy-start
  114.7 1.6 copy-start.1
  116.3 1.0 copy-start.10
  117.3 1.5 slice-start
  118.8 1.5 slice-start.1
  123.3 84.7 %copy-start.13 = (f32[256]{0:T(256)S(1)}, f32[256]{0:T(256)}, u32[]{:S(2)}) copy-start(f32[256]{0:T(256)} %param.12) | copy-start | bytes 3076
  123.3 84.7 %copy-start.14 = (f32[256]{0:T(256)S(1)}, f32[256]{0:T(256)}, u32[]{:S(2)}) copy-start(f32[256]{0:T(256)} %param.11) | copy-start | bytes 3076
  212.6 15.5 %collective-permute-start.4 = (bf16[9,1,120,256]{3,2,1,0:T(8,128)(2,1)}, bf16[9,1,120,256]{3,2,1,0:T(8,128)(2,1)S(1)}, u32[]{:S(2)}, u32[]{:S(2)}) collective-permute-start(bf16[9,1,120,256]{3,2,1,0:T(8,128)(2,1)} %slice.226), channel_id=1, source_target_pairs={{4,0},{8,4},{12,8},{16,12},{20,16},{24,20},{28,24},{5,1},{9,5},{13... | collective-permute-start | bytes 1658888 | tf_op jit(solution)/shard_map/ppermute | solution.py:30
  248.6 4.6 %copy-start.8 = (bf16[9,2,60,256]{3,2,1,0:T(8,128)(2,1)S(1)}, bf16[9,2,60,256]{3,2,1,0:T(8,128)(2,1)}, u32[]{:S(2)}) copy-start(bf16[9,2,60,256]{3,2,1,0:T(8,128)(2,1)} %slice.188) | copy-start | bytes 1658884
  248.7 9.0 %collective-permute-start.5 = (bf16[9,5,1,256]{3,2,1,0:T(2,128)(2,1)S(1)}, bf16[9,5,1,256]{3,2,1,0:T(2,128)(2,1)S(1)}, u32[]{:S(2)}, u32[]{:S(2)}) collective-permute-start(bf16[9,5,1,256]{3,2,1,0:T(2,128)(2,1)S(1)} %fusion.51), channel_id=1, source_target_pairs={{1,0},{2,1},{3,2},{5,4},{6,5},{7,6},{9,8},{10,9},{11,10},{13,12},{... | collective-permute-start | bytes 69128 | tf_op jit(solution)/shard_map/ppermute | solution.py:30
  259.7 30.7 %copy-start.2 = (bf16[9,5,121,256]{3,2,1,0:T(8,128)(2,1)S(1)}, bf16[9,5,121,256]{3,2,1,0:T(8,128)(2,1)}, u32[]{:S(2)}) copy-start(bf16[9,5,121,256]{3,2,1,0:T(8,128)(2,1)} %pad_maximum_fusion.1) | copy-start | bytes 8363524
  303.3 3.1 copy-start.9
  303.3 4.3 %copy-start.7 = (bf16[9,2,60,256]{3,2,1,0:T(8,128)(2,1)S(1)}, bf16[9,2,60,256]{3,2,1,0:T(8,128)(2,1)}, u32[]{:S(2)}) copy-start(bf16[9,2,60,256]{3,2,1,0:T(8,128)(2,1)} %slice.190) | copy-start | bytes 1658884
  304.8 4.2 %copy-start.5 = (f32[9,2,60,256]{3,2,1,0:T(8,128)S(1)}, f32[9,2,60,256]{3,2,1,0:T(8,128)}, u32[]{:S(2)}) copy-start(f32[9,2,60,256]{3,2,1,0:T(8,128)} %fusion.48) | copy-start | bytes 3317764
  304.9 4.2 %copy-start.6 = (bf16[9,2,60,256]{3,2,1,0:T(8,128)(2,1)S(1)}, bf16[9,2,60,256]{3,2,1,0:T(8,128)(2,1)}, u32[]{:S(2)}) copy-start(bf16[9,2,60,256]{3,2,1,0:T(8,128)(2,1)} %slice.184) | copy-start | bytes 1658884
  307.6 2.6 copy-start.3
  307.6 2.6 copy-start.4
  307.6 2.6 copy-start.15
Sparse Core Ops, SparseCore 0:
  9.5 52.3 all-gather.4
  64.2 39.7 all-gather.6
